TPU v7x, 512 devices: a whole 4x4x16 slice. The times are simulated.
512 devices in a mesh: ctx: 32 (over z_lo, x, core), head: 16 (over y, z_hi).
Axes of the slice: x: 4, y: 4, z: 16 (z_hi: 4, z_lo: 4; z = z_hi * 4 + z_lo), core: 2. Of those that a mesh axis runs over, the one named last changes fastest.
Arguments:
- hidden_in: bfloat16 [4096, 4096], P('ctx', 'head'), may hold values from -6 to 6
- queries: bfloat16 [4096, 4096], P('ctx', 'head'), may hold values from -16 to 16
- kv_prev: bfloat16 [4096, 2, 4096], P('ctx', None, 'head'), may hold values from -16 to 16
- norm_gain: bfloat16 [4096], replicated, may hold values from 0.099609375 to 1.8984375
- w_kv: bfloat16 [4096, 2, 4096], P(None, None, 'head'), may hold values from -0.09375 to 0.09375
- w_out: bfloat16 [4096, 4096], P('head', 'ctx'), may hold values from -0.1875 to 0.1875
Outputs:
- hidden_out: float32 [4096, 4096], P('ctx', 'head')
- kv_out: float32 [4096, 2, 4096], P('ctx', None, 'head')
All inputs are finite; a program needn't handle non-finite values.
Results may differ from a plain program's by a relative error of at most 0.033.
Values may be sent and summed in bfloat16 or wider, within the bound.
No kernel may reach another device: no remote copies, remote signals or barrier semaphores. Data moves between devices by JAX's collectives and lax.ppermute only.
A program may use at most 64 MiB of HBM per device.

v0:
```python
import jax
import jax.numpy as jnp
from jax import lax
from jax.sharding import PartitionSpec as P

D = 4096
HD = 128
ITERS = 2
MASKED = -1e30
EPSILON = 1e-05


def attend_keys(query_heads, key_value, row_start):
    row_count = query_heads.shape[0]
    head_count = query_heads.shape[1]
    score_scale = HD ** (-0.5)
    query_position = row_start + jnp.arange(row_count)
    row_last = row_start + row_count - 1
    initial = (
        jnp.full((row_count, head_count), MASKED, jnp.float32),
        jnp.zeros((row_count, head_count), jnp.float32),
        jnp.zeros((row_count, head_count, HD), jnp.float32),
    )
    incoming = lax.all_gather(key_value, "ctx", axis=0, tiled=True)

    def advance(current):
        row_max, row_sum, weighted = current
        block_rows = incoming.shape[0]
        key_block = incoming[:, 0].reshape(block_rows, head_count, HD)
        value_block = incoming[:, 1].reshape(block_rows, head_count, HD)
        scores = (
            jnp.einsum("qhd,khd->qhk", query_heads, key_block, preferred_element_type=jnp.float32)
            * score_scale
        )
        allowed = (query_position[:, None] >= jnp.arange(block_rows)[None, :])[:, None, :]
        scores = jnp.where(allowed, scores, MASKED)
        new_max = jnp.maximum(row_max, jnp.max(scores, axis=2))
        weights = jnp.where(allowed, jnp.exp(scores - new_max[:, :, None]), 0.0)
        row_sum = jnp.sum(weights, axis=2)
        weighted = jnp.einsum(
            "qhk,khd->qhd",
            weights.astype(jnp.bfloat16),
            value_block,
            preferred_element_type=jnp.float32,
        )
        return (new_max, row_sum, weighted)

    row_max, row_sum, weighted = lax.cond(
        jnp.int32(0) <= row_last, advance, lambda current: current, initial
    )
    return (weighted / row_sum[:, :, None]).astype(jnp.bfloat16).reshape(row_count, head_count * HD)


def per_device(hidden_in, queries, kv_prev, norm_gain, w_kv, w_out):
    row_count = queries.shape[0]
    local_width = queries.shape[1]
    head_count = local_width // HD
    row_start = lax.axis_index("ctx") * row_count
    column_start = lax.axis_index("head") * local_width
    out_rows = lax.all_gather(w_out, "ctx", axis=1, tiled=True)
    kv_weights = w_kv.reshape(w_kv.shape[0], 2 * local_width)
    gain_all = norm_gain.astype(jnp.float32)
    gain_here = lax.dynamic_slice_in_dim(gain_all, column_start, local_width)
    query_heads = queries.reshape(row_count, head_count, HD)
    input_here = hidden_in.astype(jnp.float32)
    key_value = kv_prev
    for iteration in range(ITERS):
        attended = attend_keys(query_heads, key_value, row_start)
        partial_value = jnp.dot(attended, out_rows, preferred_element_type=jnp.float32)
        branch_sum = lax.psum_scatter(
            partial_value.astype(jnp.bfloat16), "head", scatter_dimension=1, tiled=True
        ).astype(jnp.float32)
        hidden = input_here + branch_sum
        squares = lax.psum(jnp.sum(hidden * hidden, axis=1), "head")
        normed = (hidden * lax.rsqrt(squares / D + EPSILON)[:, None] * gain_here).astype(
            jnp.bfloat16
        )
        fresh_kv = jnp.dot(
            lax.all_gather(normed, "head", axis=1, tiled=True),
            kv_weights,
            preferred_element_type=jnp.float32,
        )
        hidden_out = hidden
        kv_product = fresh_kv.reshape(row_count, 2, local_width)
        key_value = kv_product.astype(jnp.bfloat16)
    return (hidden_out, kv_product)


def solution(mesh):
    in_specs = (
        P("ctx", "head"),
        P("ctx", "head"),
        P("ctx", None, "head"),
        P(),
        P(None, None, "head"),
        P("head", "ctx"),
    )
    out_specs = (P("ctx", "head"), P("ctx", None, "head"))
    return jax.shard_map(
        per_device, mesh=mesh, in_specs=in_specs, out_specs=out_specs, check_vma=False
    )
```

profile of v0, /device:TPU:97, one launch (start us, length us, event | category | flops | bytes accessed | tf_op | source)
XLA Modules:
  0.0 747.0 jit_solution(11621251483294013254)
XLA Ops:
  7.2 0.0 all-gather.6.cloned.1.call-start
  7.2 1.7 copy.38
  8.9 0.0 all-gather.6.cloned.1.call-update
  8.9 0.0 all-gather.8.cloned.1.call-start
  9.0 0.7 all-gather.8.cloned.1.call-update
  9.7 0.0 reduce-scatter.3.cloned.1.call-start
  9.7 1.0 copy.39
  10.7 77.8 %all-gather.6.cloned.1.call-done = bf16[4096,2,256]{0,2,1:T(8,128)(2,1)} async-done(((bf16[128,2,256]{0,2,1:T(8,128)(2,1)}), bf16[4096,2,256]{0,2,1:T(8,128)(2,1)}) %all-gather.6.cloned.1.call-update) | async-done | bytes 4194320 | tf_op jit(solution)/shard_map/all_gather | solution.py:24
  88.5 6.9 conditional.2
  88.5 0.3 iota_compare_fusion
  88.9 2.7 fusion.29
  91.6 1.3 fusion.30
  92.9 1.5 fusion.9
  94.5 0.8 fusion.3
  95.3 0.1 copy.56
  95.4 0.0 copy-start.1
  95.4 62.8 %all-gather.8.cloned.1.call-done = bf16[256,4096]{1,0:T(8,128)(2,1)} async-done(((bf16[256,128]{1,0:T(8,128)(2,1)}), bf16[256,4096]{1,0:T(8,128)(2,1)}) %all-gather.8.cloned.1.call-update) | async-done | bytes 2097168 | tf_op jit(solution)/shard_map/all_gather | solution.py:60
  158.3 3.0 convolution_convert_fusion.1
  161.3 0.0 reduce-scatter.3.cloned.1.call-update
  161.3 0.0 all-gather.10.cloned.1.call-start
  161.4 0.8 dynamic-slice_convert_fusion
  162.1 110.8 %reduce-scatter.3.cloned.1.call-done = bf16[128,256]{1,0:T(8,128)(2,1)} async-done(((bf16[128,4096]{1,0:T(8,128)(2,1)}), bf16[128,256]{1,0:T(8,128)(2,1)}) %reduce-scatter.3.cloned.1.call-update) | async-done | bytes 65552 | tf_op jit(solution)/shard_map/reduce_scatter | solution.py:70
  272.9 0.0 copy-done.1
  272.9 0.9 multiply_reduce_fusion.1
  273.9 44.0 %psum.14 = f32[128]{0:T(128)S(1)} all-reduce(f32[128]{0:T(128)S(1)} %multiply_reduce_fusion.1), channel_id=1, replica_groups=mesh['ctx'=32,'head'=16] {'head'}, use_global_device_ids=true, to_apply=%region_6.7 | all-reduce | flops 128 | bytes 1024 | tf_op jit(solution)/shard_map/psum | solution.py:74
  317.9 1.6 multiply_convert_fusion.1
  319.4 0.0 all-gather.10.cloned.1.call-update
  319.5 0.0 all-gather.12.cloned.1.call-start
  319.5 4.9 copy.59
  324.4 6.4 copy.42
  330.8 78.9 %all-gather.10.cloned.1.call-done = bf16[128,4096]{1,0:T(8,128)(2,1)} async-done(((bf16[128,256]{1,0:T(8,128)(2,1)}), bf16[128,4096]{1,0:T(8,128)(2,1)}) %all-gather.10.cloned.1.call-update) | async-done | bytes 1048592 | tf_op jit(solution)/shard_map/all_gather | solution.py:79
  409.7 4.7 convolution_convert_fusion.2
  414.4 0.0 all-gather.12.cloned.1.call-update
  414.4 0.2 reduce-scatter.5.cloned.1.call-start
  414.6 59.2 %all-gather.12.cloned.1.call-done = bf16[4096,2,256]{2,0,1:T(8,128)(2,1)} async-done(((bf16[128,2,256]{2,0,1:T(8,128)(2,1)}), bf16[4096,2,256]{2,0,1:T(8,128)(2,1)}) %all-gather.12.cloned.1.call-update) | async-done | bytes 4194320 | tf_op jit(solution)/shard_map/all_gather | solution.py:24
  473.8 0.0 copy-start
  473.8 13.5 %conditional.3 = (f32[128,2]{0,1:T(2,128)S(1)}, f32[128,2,128]{0,2,1:T(8,128)S(1)}) conditional(s32[]{:T(128)} %convert_element_type.44, () %tuple.24, (s32[128]{0:T(128)S(1)}, bf16[4096,2,256]{2,0,1:T(8,128)(2,1)}, bf16[128,2,128]{0,2,1:T(8,128)(2,1)S(1)}) %tuple.65), branch_computations={%region_7.8_spmd, %region_8.11_spmd} | conditional | flops 546832128 | bytes 36117008 | solution.py:48
  473.8 0.3 iota_compare_fusion.1
  474.2 6.6 copy.43
  480.8 2.7 fusion.31
  483.5 1.3 fusion.32
  484.8 1.5 fusion.22
  486.3 0.8 fusion.16
  487.2 0.1 copy.58
  487.3 0.0 copy-done
  487.3 1.4 convolution_convert_fusion
  488.8 0.0 reduce-scatter.5.cloned.1.call-update
  488.8 0.0 all-gather.14.cloned.1.call-start
  488.9 110.3 %reduce-scatter.5.cloned.1.call-done = bf16[128,256]{1,0:T(8,128)(2,1)} async-done(((bf16[128,4096]{1,0:T(8,128)(2,1)}), bf16[128,256]{1,0:T(8,128)(2,1)}) %reduce-scatter.5.cloned.1.call-update) | async-done | bytes 65552 | tf_op jit(solution)/shard_map/reduce_scatter | solution.py:70
  599.2 0.9 multiply_reduce_fusion
  600.1 0.0 copy-start.2
  600.1 44.1 %psum.15 = f32[128]{0:T(128)S(1)} all-reduce(f32[128]{0:T(128)S(1)} %get-tuple-element.51), channel_id=1, replica_groups=mesh['ctx'=32,'head'=16] {'head'}, use_global_device_ids=true, to_apply=%region_13.14 | all-reduce | flops 128 | bytes 1024 | tf_op jit(solution)/shard_map/psum | solution.py:74
  644.2 0.7 multiply_convert_fusion
  644.9 0.0 all-gather.14.cloned.1.call-update
  644.9 90.2 %all-gather.14.cloned.1.call-done = bf16[128,4096]{1,0:T(8,128)(2,1)} async-done(((bf16[128,256]{1,0:T(8,128)(2,1)}), bf16[128,4096]{1,0:T(8,128)(2,1)}) %all-gather.14.cloned.1.call-update) | async-done | bytes 1048592 | tf_op jit(solution)/shard_map/all_gather | solution.py:79
  735.1 4.0 fusion.26
  739.2 0.9 copy.46
  740.1 0.0 copy-done.2
  (7 shorter events, 0.1 us)
Async XLA Ops:
  7.2 81.4 %all-gather.6.cloned.1.call-start = ((), (), s32[]{:S(2)}) async-start(), calls=%async_computation.2 | async-start | bytes 4325376 | tf_op jit(solution)/shard_map/all_gather | solution.py:24
  8.9 149.4 %all-gather.8.cloned.1.call-start = ((), (), s32[]{:S(2)}) async-start(), calls=%async_computation.3 | async-start | bytes 2162688 | tf_op jit(solution)/shard_map/all_gather | solution.py:60
  9.7 263.2 %reduce-scatter.3.cloned.1.call-start = ((), (), s32[]{:S(2)}) async-start(), calls=%async_computation.4 | async-start | bytes 1114112 | tf_op jit(solution)/shard_map/reduce_scatter | solution.py:70
  95.4 177.5 %copy-start.1 = (bf16[128,256]{1,0:T(8,128)(2,1)S(1)}, bf16[128,256]{1,0:T(8,128)(2,1)}, u32[]{:S(2)}) copy-start(bf16[128,256]{1,0:T(8,128)(2,1)} %param.10) | copy-start | bytes 196612
  161.3 248.3 %all-gather.10.cloned.1.call-start = ((), (), s32[]{:S(2)}) async-start(), calls=%async_computation.5 | async-start | bytes 1114112 | tf_op jit(solution)/shard_map/all_gather | solution.py:79
  319.5 154.4 %all-gather.12.cloned.1.call-start = ((), (), s32[]{:S(2)}) async-start(), calls=%async_computation.6 | async-start | bytes 4325376 | tf_op jit(solution)/shard_map/all_gather | solution.py:24
  414.4 184.8 %reduce-scatter.5.cloned.1.call-start = ((), (), s32[]{:S(2)}) async-start(), calls=%async_computation.7 | async-start | bytes 1114112 | tf_op jit(solution)/shard_map/reduce_scatter | solution.py:70
  473.8 13.5 %copy-start = (bf16[256,4096]{1,0:T(8,128)(2,1)S(1)}, bf16[256,4096]{1,0:T(8,128)(2,1)}, u32[]{:S(2)}) copy-start(bf16[256,4096]{1,0:T(8,128)(2,1)} %all-gather.8.cloned.1.call-done) | copy-start | bytes 6291460
  488.8 246.3 %all-gather.14.cloned.1.call-start = ((), (), s32[]{:S(2)}) async-start(), calls=%async_computation.8 | async-start | bytes 1114112 | tf_op jit(solution)/shard_map/all_gather | solution.py:79
  600.1 140.0 %copy-start.2 = (f32[128,256]{1,0:T(8,128)}, f32[128,256]{1,0:T(8,128)S(1)}, u32[]{:S(2)}) copy-start(f32[128,256]{1,0:T(8,128)S(1)} %get-tuple-element.52) | copy-start | bytes 393220
Sparse Core Ops, SparseCore 0:
  10.6 77.8 all-gather.5
  90.6 67.6 all-gather.7
  162.4 110.4 reduce-scatter.2
  319.6 90.0 all-gather.9
  414.5 59.2 all-gather.11
  488.9 110.1 reduce-scatter.4
  645.1 90.0 all-gather.13
where the time goes:
time: 748 us; the launch traced here: 747 us
  waiting for transfers between devices  591 us (79%)
  blocking collectives  88.1 us (12%)
  local copies, waits for them, and re-layouts  27 us (4%)
  matrix products  18.9 us (3%)
  between operations  14.2 us (2%)
    reduce_scatter x2, waiting for transfers between devices, per_device(): lax.psum_scatter(partial_value.astype(jnp.bfloat16), 'head', scatter_dime...  221 us
    all_gather x2, waiting for transfers between devices, per_device(): lax.all_gather(normed, 'head', axis=1, tiled=True)  169 us
    all_gather x2, waiting for transfers between devices, attend_keys(): incoming = lax.all_gather(key_value, 'ctx', axis=0, tiled=True)  137 us
    psum x2, blocking collectives, per_device(): squares = lax.psum(jnp.sum(hidden * hidden, axis=1), 'head')  88.1 us
    all_gather x1, waiting for transfers between devices, per_device(): out_rows = lax.all_gather(w_out, 'ctx', axis=1, tiled=True)  62.8 us
  transfers between devices with their start and end apart: 7, of which 7 were waited for; matrix products, arithmetic and copies ran while one was open for 3% of the time, Pallas kernels for 0%

commit v1 on v0

--- a/solution.py
+++ b/solution.py
@@ -76,7 +76,9 @@
             jnp.bfloat16
         )
         fresh_kv = jnp.dot(
-            lax.all_gather(normed, "head", axis=1, tiled=True),
+            jnp.concatenate(
+                lax.all_to_all(jnp.stack([normed] * lax.axis_size("head")), "head", 0, 0), axis=1
+            ),
             kv_weights,
             preferred_element_type=jnp.float32,
         )

time: 748 us -> 694 us (0.928)
  the two profiles are of different devices: /device:TPU:97 before, /device:TPU:4 now
where the time goes in v1:
time: 694 us; the launch traced here: 693 us
  waiting for transfers between devices  466 us (67%)
  blocking collectives  154 us (22%)
  local copies, waits for them, and re-layouts  30.5 us (4%)
  matrix products  18.3 us (3%)
  between operations  13.9 us (2%)
    reduce_scatter x2, waiting for transfers between devices, per_device(): lax.psum_scatter(partial_value.astype(jnp.bfloat16), 'head', scatter_dime...  231 us
    all_gather x2, waiting for transfers between devices, attend_keys(): incoming = lax.all_gather(key_value, 'ctx', axis=0, tiled=True)  137 us
    psum x2, blocking collectives, per_device(): squares = lax.psum(jnp.sum(hidden * hidden, axis=1), 'head')  104 us
    all_gather x1, waiting for transfers between devices, per_device(): out_rows = lax.all_gather(w_out, 'ctx', axis=1, tiled=True)  62.8 us
    all_to_all x1, blocking collectives, per_device(): lax.all_to_all(jnp.stack([normed] * lax.axis_size('head')), 'head', 0, 0)  50.2 us
    all_to_all x1, waiting for transfers between devices, per_device(): lax.all_to_all(jnp.stack([normed] * lax.axis_size('head')), 'head', 0, 0)  34.5 us
  transfers between devices with their start and end apart: 6, of which 6 were waited for; matrix products, arithmetic and copies ran while one was open for 3% of the time, Pallas kernels for 0%

profile of v1, /device:TPU:4, one launch (start us, length us, event | category | flops | bytes accessed | tf_op | source)
XLA Modules:
  0.0 693.4 jit_solution(10020664413431481304)
XLA Ops:
  7.2 0.0 all-gather.4.cloned.1.call-start
  7.2 1.7 copy.38
  8.9 0.0 all-gather.4.cloned.1.call-update
  8.9 0.0 all-gather.6.cloned.1.call-start
  9.0 0.7 all-gather.6.cloned.1.call-update
  9.7 0.0 reduce-scatter.3.cloned.1.call-start
  9.7 1.0 copy.39
  10.7 79.1 %all-gather.4.cloned.1.call-done = bf16[4096,2,256]{0,2,1:T(8,128)(2,1)} async-done(((bf16[128,2,256]{0,2,1:T(8,128)(2,1)}), bf16[4096,2,256]{0,2,1:T(8,128)(2,1)}) %all-gather.4.cloned.1.call-update) | async-done | bytes 4194320 | tf_op jit(solution)/shard_map/all_gather | solution.py:24
  89.8 6.9 conditional.2
  89.8 0.3 iota_compare_fusion
  90.1 2.7 fusion.26
  92.9 1.3 fusion.27
  94.2 1.5 fusion.9
  95.7 0.8 fusion.3
  96.6 0.1 copy.58
  96.7 0.0 copy-start.1
  96.7 62.8 %all-gather.6.cloned.1.call-done = bf16[256,4096]{1,0:T(8,128)(2,1)} async-done(((bf16[256,128]{1,0:T(8,128)(2,1)}), bf16[256,4096]{1,0:T(8,128)(2,1)}) %all-gather.6.cloned.1.call-update) | async-done | bytes 2097168 | tf_op jit(solution)/shard_map/all_gather | solution.py:60
  159.5 3.1 convolution_convert_fusion.1
  162.6 0.0 reduce-scatter.3.cloned.1.call-update
  162.6 0.8 dynamic-slice_convert_fusion
  163.4 115.5 %reduce-scatter.3.cloned.1.call-done = bf16[128,256]{1,0:T(8,128)(2,1)} async-done(((bf16[128,4096]{1,0:T(8,128)(2,1)}), bf16[128,256]{1,0:T(8,128)(2,1)}) %reduce-scatter.3.cloned.1.call-update) | async-done | bytes 65552 | tf_op jit(solution)/shard_map/reduce_scatter | solution.py:70
  278.9 0.0 copy-done.1
  278.9 0.9 multiply_reduce_fusion.1
  279.8 51.7 %psum.14 = f32[128]{0:T(128)S(1)} all-reduce(f32[128]{0:T(128)S(1)} %multiply_reduce_fusion.1), channel_id=1, replica_groups=mesh['ctx'=32,'head'=16] {'head'}, use_global_device_ids=true, to_apply=%region_6.7 | all-reduce | flops 128 | bytes 1024 | tf_op jit(solution)/shard_map/psum | solution.py:74
  331.5 0.9 multiply_convert_fusion.1
  332.5 1.2 stack.4
  333.6 4.7 all-to-all-start
  338.3 0.0 all-gather.8.cloned.1.call-start
  338.4 4.9 copy.61
  343.2 6.4 copy.43
  349.7 34.5 %all-to-all-done = bf16[16,128,256]{2,1,0:T(8,128)(2,1)S(1)} async-done(((bf16[16,128,256]{2,1,0:T(8,128)(2,1)}), bf16[16,128,256]{2,1,0:T(8,128)(2,1)S(1)}, u32[]{:S(2)}, u32[]{:S(2)}) %all-to-all-start) | async-done | bytes 1048608 | tf_op jit(solution)/shard_map/all_to_all | solution.py:80
  384.1 0.6 copy.42
  384.7 0.5 reshape.89
  385.3 4.4 convolution_convert_fusion.2
  389.6 0.0 all-gather.8.cloned.1.call-update
  389.7 0.2 reduce-scatter.5.cloned.1.call-start
  389.9 57.9 %all-gather.8.cloned.1.call-done = bf16[4096,2,256]{2,0,1:T(8,128)(2,1)} async-done(((bf16[128,2,256]{2,0,1:T(8,128)(2,1)}), bf16[4096,2,256]{2,0,1:T(8,128)(2,1)}) %all-gather.8.cloned.1.call-update) | async-done | bytes 4194320 | tf_op jit(solution)/shard_map/all_gather | solution.py:24
  447.8 0.0 copy-start
  447.8 13.5 %conditional.3 = (f32[128,2]{0,1:T(2,128)S(1)}, f32[128,2,128]{0,2,1:T(8,128)S(1)}) conditional(s32[]{:T(128)} %convert_element_type.44, () %tuple.24, (s32[128]{0:T(128)S(1)}, bf16[4096,2,256]{2,0,1:T(8,128)(2,1)}, bf16[128,2,128]{0,2,1:T(8,128)(2,1)S(1)}) %tuple.61), branch_computations={%region_7.8_spmd, %region_8.11_spmd} | conditional | flops 546832128 | bytes 36117008 | solution.py:48
  447.8 0.3 iota_compare_fusion.1
  448.1 6.6 copy.44
  454.7 2.7 fusion.28
  457.5 1.3 fusion.29
  458.8 1.5 fusion.22
  460.3 0.8 fusion.16
  461.2 0.1 copy.60
  461.3 0.0 copy-done
  461.3 1.4 convolution_convert_fusion
  462.8 0.0 reduce-scatter.5.cloned.1.call-update
  462.8 115.1 %reduce-scatter.5.cloned.1.call-done = bf16[128,256]{1,0:T(8,128)(2,1)} async-done(((bf16[128,4096]{1,0:T(8,128)(2,1)}), bf16[128,256]{1,0:T(8,128)(2,1)}) %reduce-scatter.5.cloned.1.call-update) | async-done | bytes 65552 | tf_op jit(solution)/shard_map/reduce_scatter | solution.py:70
  577.9 0.9 multiply_reduce_fusion
  578.9 0.0 copy-start.2
  578.9 51.8 %psum.15 = f32[128]{0:T(128)S(1)} all-reduce(f32[128]{0:T(128)S(1)} %get-tuple-element.51), channel_id=1, replica_groups=mesh['ctx'=32,'head'=16] {'head'}, use_global_device_ids=true, to_apply=%region_13.14 | all-reduce | flops 128 | bytes 1024 | tf_op jit(solution)/shard_map/psum | solution.py:74
  630.7 0.1 multiply_convert_fusion
  630.8 0.1 stack.5
  630.9 50.2 %all_to_all.10 = bf16[16,128,256]{2,1,0:T(8,128)(2,1)S(1)} all-to-all(bf16[16,128,256]{2,1,0:T(8,128)(2,1)S(1)} %stack.5), channel_id=1, replica_groups=mesh['ctx'=32,'head'=16] {'head'}, dimensions={0} | all-to-all | bytes 2097152 | tf_op jit(solution)/shard_map/all_to_all | solution.py:80
  681.1 0.6 copy.47
  681.7 0.5 reshape.90
  682.2 3.7 fusion.30
  685.9 0.0 copy-done.2
  686.0 0.9 copy.48
  (7 shorter events, 0.1 us)
Async XLA Ops:
  7.2 82.6 %all-gather.4.cloned.1.call-start = ((), (), s32[]{:S(2)}) async-start(), calls=%async_computation.4 | async-start | bytes 4325376 | tf_op jit(solution)/shard_map/all_gather | solution.py:24
  8.9 150.6 %all-gather.6.cloned.1.call-start = ((), (), s32[]{:S(2)}) async-start(), calls=%async_computation.5 | async-start | bytes 2162688 | tf_op jit(solution)/shard_map/all_gather | solution.py:60
  9.7 269.2 %reduce-scatter.3.cloned.1.call-start = ((), (), s32[]{:S(2)}) async-start(), calls=%async_computation.6 | async-start | bytes 1114112 | tf_op jit(solution)/shard_map/reduce_scatter | solution.py:70
  96.7 182.2 %copy-start.1 = (bf16[128,256]{1,0:T(8,128)(2,1)S(1)}, bf16[128,256]{1,0:T(8,128)(2,1)}, u32[]{:S(2)}) copy-start(bf16[128,256]{1,0:T(8,128)(2,1)} %param.10) | copy-start | bytes 196612
  333.6 50.5 %all-to-all-start = ((bf16[16,128,256]{2,1,0:T(8,128)(2,1)}), bf16[16,128,256]{2,1,0:T(8,128)(2,1)S(1)}, u32[]{:S(2)}, u32[]{:S(2)}) async-start(bf16[16,128,256]{2,1,0:T(8,128)(2,1)} %stack.4), calls=%async_computation.1 | async-start | bytes 2097152 | tf_op jit(solution)/shard_map/all_to_all | solution.py:80
  338.3 109.5 %all-gather.8.cloned.1.call-start = ((), (), s32[]{:S(2)}) async-start(), calls=%async_computation.7 | async-start | bytes 4325376 | tf_op jit(solution)/shard_map/all_gather | solution.py:24
  389.7 188.3 %reduce-scatter.5.cloned.1.call-start = ((), (), s32[]{:S(2)}) async-start(), calls=%async_computation.8 | async-start | bytes 1114112 | tf_op jit(solution)/shard_map/reduce_scatter | solution.py:70
  447.8 13.5 %copy-start = (bf16[256,4096]{1,0:T(8,128)(2,1)S(1)}, bf16[256,4096]{1,0:T(8,128)(2,1)}, u32[]{:S(2)}) copy-start(bf16[256,4096]{1,0:T(8,128)(2,1)} %all-gather.6.cloned.1.call-done) | copy-start | bytes 6291460
  578.9 107.1 %copy-start.2 = (f32[128,256]{1,0:T(8,128)}, f32[128,256]{1,0:T(8,128)S(1)}, u32[]{:S(2)}) copy-start(f32[128,256]{1,0:T(8,128)S(1)} %get-tuple-element.52) | copy-start | bytes 393220
Sparse Core Ops, SparseCore 0:
  10.6 79.1 all-gather.3
  91.9 67.6 all-gather.5
  163.6 115.1 reduce-scatter.2
  389.8 57.9 all-gather.7
  462.9 114.9 reduce-scatter.4
